TPU v7x, 128 devices: a whole 4x4x4 slice. The times are simulated.
128 devices in a mesh: depth: 4 (over x), probe: 32 (over z, y, core).
Axes of the slice: x: 4, y: 4, z: 4, core: 2. Of those that a mesh axis runs over, the one named last changes fastest.
Arguments:
- atom_blocks: bfloat16 [4, 4096, 128, 128], P('depth', 'probe'), may hold values from 0 to 1.5
- atom_tile: int32 [4, 4096], P('depth', 'probe'), may hold values from 0 to 1023, as said below
- slice_counts: int32 [4], P('depth'), may hold values from 1 to 4, as said below
- positions: int32 [128], P('probe'), may hold values from 0 to 7, as said below
- probe_wave: float32 [2, 256, 256], replicated, may hold values from -4 to 4
- prop_phase: float32 [256, 256], replicated, may hold values from -3.140625 to 3.140625
Outputs:
- exit_waves: float32 [4, 128, 2, 256, 256], P('depth', 'probe')
Inputs may be any that keep to these rules, and one draw needn't show every extreme that they name: `atom_tile`: tile number owner * 32 + s * 8 + c names tile row owner, slice slot s and tile column c, with s below slice_counts of that section. In each section the 128 atoms of one index of probe (aligned blocks) name at most 6 tiles of any one tile row, and in every draw each section has a tile row that receives exactly 6 from every such block. `slice_counts`: some section has exactly 4 slices in every draw. The 4 probes of one tile row (aligned blocks of 4) have distinct positions.
All inputs are finite; a program needn't handle non-finite values.
Results may differ from a plain program's by a relative error of at most 0.04.
Values may be sent and summed in bfloat16 or wider, within the bound.
No kernel may reach another device: no remote copies, remote signals or barrier semaphores. Data moves between devices by JAX's collectives and lax.ppermute only.
A program may use at most 128 MiB of HBM per device.

v0:
```python
import math

import jax
import jax.numpy as jnp
from jax import lax
from jax.sharding import PartitionSpec as P

SLICE_MAX = 4
TCOLS = 8


SIGMA = 0.7


def extended_2(x, sides, width):
    for axis, dim in sides:
        devices, length = (lax.axis_size(axis), x.shape[dim])
        up = [(i, (i + 1) % devices) for i in range(devices)]
        down = [(j, i) for i, j in up]
        last = lax.slice_in_dim(x, length - width, length, axis=dim)
        first = lax.slice_in_dim(x, 0, width, axis=dim)
        before = lax.ppermute(last, axis, up)
        after = lax.ppermute(first, axis, down)
        x = jnp.concatenate([before, x, after], axis=dim)
    return x


def shifted(block, axis, distance):
    devices = range(lax.axis_size(axis))
    route = [(i - distance, i) for i in devices if i - distance in devices]
    return lax.ppermute(block, axis, route)


def dft_tables(points):
    grid_index = jnp.arange(points, dtype=jnp.int32)
    angle_table = (grid_index[:, None] * grid_index[None, :] % points).astype(jnp.float32) * (
        2.0 * math.pi / points
    )
    norm_scale = 1.0 / math.sqrt(points)
    real_part = (jnp.cos(angle_table) * norm_scale).astype(jnp.bfloat16)
    imag_part = (-jnp.sin(angle_table) * norm_scale).astype(jnp.bfloat16)
    return (real_part, imag_part)


def left_apply(real_part, imag_part, field):
    first_term = jnp.einsum("jk,bckl->bcjl", real_part, field, preferred_element_type=jnp.float32)
    second_term = jnp.einsum("jk,bckl->bcjl", imag_part, field, preferred_element_type=jnp.float32)
    return jnp.stack(
        [first_term[:, 0] - second_term[:, 1], first_term[:, 1] + second_term[:, 0]], axis=1
    )


def right_apply(real_part, imag_part, field):
    first_term = jnp.einsum("bcjk,kl->bcjl", field, real_part, preferred_element_type=jnp.float32)
    second_term = jnp.einsum("bcjk,kl->bcjl", field, imag_part, preferred_element_type=jnp.float32)
    return jnp.stack(
        [first_term[:, 0] - second_term[:, 1], first_term[:, 1] + second_term[:, 0]], axis=1
    )


def slice_step(wave, cropped, real_part, imag_part, rotor_cos, rotor_sin):
    cosine = jnp.cos(SIGMA * cropped)
    sine_part = jnp.sin(SIGMA * cropped)
    wave_re = wave[:, 0]
    wave_im = wave[:, 1]
    passed = jnp.stack(
        [wave_re * cosine - wave_im * sine_part, wave_re * sine_part + wave_im * cosine], axis=1
    ).astype(jnp.bfloat16)
    spectrum = left_apply(real_part, imag_part, passed).astype(jnp.bfloat16)
    spectral = right_apply(real_part, imag_part, spectrum)
    propagated = jnp.stack(
        [
            spectral[:, 0] * rotor_cos - spectral[:, 1] * rotor_sin,
            spectral[:, 0] * rotor_sin + spectral[:, 1] * rotor_cos,
        ],
        axis=1,
    ).astype(jnp.bfloat16)
    returned = left_apply(real_part, -imag_part, propagated).astype(jnp.bfloat16)
    return right_apply(real_part, -imag_part, returned)


def assemble(blocks, slot_tiles, tiles_dev, tile_cols):
    slot_count, height, tile_size = blocks.shape
    member = (slot_tiles[:, None] == jnp.arange(tiles_dev, dtype=jnp.int32)[None, :]).astype(
        jnp.bfloat16
    )
    summed = jnp.einsum(
        "st,sk->tk",
        member,
        blocks.reshape(slot_count, height * tile_size),
        preferred_element_type=jnp.float32,
    )
    summed = summed.reshape(tiles_dev // tile_cols, tile_cols, height, tile_size)
    return summed.transpose(0, 2, 1, 3).reshape(
        tiles_dev // tile_cols, height, tile_cols * tile_size
    )


def shards(atom_blocks, atom_tile, slice_counts, positions, probe_wave, prop_phase):
    owners = lax.axis_size("probe")
    sections = lax.axis_size("depth")
    depth_index = lax.axis_index("depth")
    tile_size = atom_blocks.shape[-1]
    half_tile = tile_size // 2
    window = 2 * tile_size
    atoms_dev = atom_blocks.shape[1]
    capacity = max(2, 3 * atoms_dev // (2 * owners))
    tiles_dev = SLICE_MAX * TCOLS
    blocks = atom_blocks[0]
    targets = atom_tile[0]
    owner_of = targets // tiles_dev
    local_tile = targets % tiles_dev
    member = (owner_of[:, None] == jnp.arange(owners, dtype=jnp.int32)[None, :]).astype(jnp.int32)
    group_rank = jnp.sum(jnp.cumsum(member, axis=0) * member, axis=1) - 1
    slot_own = owner_of * capacity + group_rank
    empty_ids = jnp.full((owners * capacity,), -1, jnp.int32)
    outgoing = (
        jnp.zeros((owners * capacity, tile_size, tile_size), jnp.bfloat16).at[slot_own].set(blocks)
    )
    own_ids = empty_ids.at[slot_own].set(local_tile)
    arrived, arrived_tiles = (
        lax.all_to_all(outgoing, "probe", split_axis=0, concat_axis=0, tiled=True),
        lax.all_to_all(own_ids, "probe", split_axis=0, concat_axis=0, tiled=True),
    )
    stripe = assemble(arrived, arrived_tiles, tiles_dev, TCOLS)
    extended = extended_2(stripe, (("probe", 1),), half_tile)
    wrapped = jnp.concatenate([extended, extended[:, :, :tile_size]], axis=2)
    real_part, imag_part = dft_tables(window)
    rotor_cos = jnp.cos(prop_phase)
    rotor_sin = jnp.sin(prop_phase)
    slice_count = slice_counts[0]
    waves_dev = positions.shape[0]
    per_batch = 2
    batches = waves_dev // per_batch

    def crop_all(slice_index, offsets):
        plane = lax.dynamic_index_in_dim(wrapped, slice_index, 0, keepdims=False)

        def crop_one(offset):
            return lax.dynamic_slice(plane, (jnp.int32(0), offset * tile_size), (window, window))

        return jax.vmap(crop_one)(offsets)

    def run_section(entering, offsets):

        def one_slice(slice_index, wave):
            return slice_step(
                wave, crop_all(slice_index, offsets), real_part, imag_part, rotor_cos, rotor_sin
            )

        return lax.fori_loop(0, slice_count, one_slice, entering)

    def skip_section(entering, offsets):
        return entering

    launched = jnp.broadcast_to(probe_wave[None], (per_batch, 2, window, window))
    carried = jnp.zeros_like(launched)
    results = jnp.zeros((waves_dev, 2, window, window), jnp.float32)
    step_total = batches + sections - 1
    for step_index in range(step_total):
        micro_index = step_index - depth_index
        active = (micro_index >= 0) & (micro_index < batches)
        batch_start = jnp.clip(micro_index, 0, batches - 1) * per_batch
        offsets = lax.dynamic_slice_in_dim(positions, batch_start, per_batch)
        entering = jnp.where(depth_index == 0, launched, carried)
        leaving = lax.cond(active, run_section, skip_section, entering, offsets)
        updated = lax.dynamic_update_slice_in_dim(results, leaving, batch_start, 0)
        results = jnp.where(active, updated, results)
        if step_index + 1 < step_total:
            carried = shifted(leaving, "depth", 1)
    return results[None]


def solution(mesh):
    in_specs = (
        P("depth", "probe", None, None),
        P("depth", "probe"),
        P("depth"),
        P("probe"),
        P(),
        P(),
    )
    out_specs = P("depth", "probe", None, None, None)
    return jax.shard_map(shards, mesh=mesh, in_specs=in_specs, out_specs=out_specs, check_vma=False)
```

profile of v0, /device:TPU:22, one launch (start us, length us, event | category | flops | bytes accessed | tf_op | source)
XLA Modules:
  0.0 465.6 jit_solution(10222199236644744177)
XLA Ops:
  3.5 8.4 %all-to-all-start = ((s32[32,6,1]{1,2,0:T(1,128)}), s32[32,6,1]{1,2,0:T(1,128)S(1)}, u32[]{:S(2)}, u32[]{:S(2)}) async-start(s32[32,6,1]{1,2,0:T(1,128)} %bitcast.125), calls=%async_computation | async-start | bytes 32768 | tf_op jit(solution)/shard_map/all_to_all | solution.py:123
  11.9 4.3 broadcast_in_dim.26
  16.2 19.3 %scatter_fusion = bf16[192,128,128]{2,1,0:T(8,128)(2,1)} fusion(bf16[192,128,128]{2,1,0:T(8,128)(2,1)} %broadcast_in_dim.26, s32[128]{0:T(128)S(1)} %fusion.154, bf16[128,128,128]{2,1,0:T(8,128)(2,1)} %bitcast.613), kind=kCustom, calls=%fused_computation.1 | custom fusion | bytes 12583424 | tf_op jit(solution)/shard_map/scatter | solution.py:118
  35.5 7.5 %all-to-all-start.1 = ((bf16[192,128,128]{2,1,0:T(8,128)(2,1)}), bf16[192,128,128]{2,1,0:T(8,128)(2,1)}, u32[]{:S(2)}, u32[]{:S(2)}) async-start(bf16[192,128,128]{2,1,0:T(8,128)(2,1)} %scatter_fusion), calls=%async_computation.1 | async-start | bytes 12582912 | tf_op jit(solution)/shard_map/all_to_all | solution.py:122
  44.3 72.3 %all-to-all-done.1 = bf16[192,128,128]{2,1,0:T(8,128)(2,1)} async-done(((bf16[192,128,128]{2,1,0:T(8,128)(2,1)}), bf16[192,128,128]{2,1,0:T(8,128)(2,1)}, u32[]{:S(2)}, u32[]{:S(2)}) %all-to-all-start.1) | async-done | bytes 6291488 | tf_op jit(solution)/shard_map/all_to_all | solution.py:122
  116.6 7.8 %fusion.142 = f32[4,128,8,128]{3,2,1,0:T(8,128)} fusion(s32[4,8]{1,0:T(4,128)S(1)} %multiply_add_fusion, s32[192]{0:T(256)S(1)} %eq.59, bf16[24,8,128,128]{3,2,1,0:T(8,128)(2,1)} %bitcast.187), kind=kOutput, calls=%fused_computation.297 | convolution fusion | flops 201332736 | bytes 8389504 | tf_op jit(solution)/shard_map/st,sk->tk/dot_general | solution.py:87
  124.4 1.7 reshape.357
  126.1 1.5 fusion.157
  127.6 1.9 collective-permute-start.1
  129.5 1.1 multiply_convert_fusion
  130.6 1.9 fusion.158
  132.6 9.8 %collective-permute-done = f32[4,64,1024]{2,1,0:T(8,128)} collective-permute-done((f32[4,64,1024]{2,1,0:T(8,128)}, f32[4,64,1024]{2,1,0:T(8,128)}, u32[]{:S(2)}, u32[]{:S(2)}) %collective-permute-start) | collective-permute-done | bytes 1048608 | tf_op jit(solution)/shard_map/ppermute | solution.py:22
  142.3 1.3 constant_dynamic-update-slice_fusion.7
  143.8 1.3 constant_dynamic-update-slice_fusion.5
  145.2 2.6 pad_maximum_fusion.65
  148.1 1.3 collective-permute-start.2
  149.4 26.5 %collective-permute-done.2 = f32[2,2,256,256]{3,2,1,0:T(8,128)} collective-permute-done((f32[2,2,256,256]{3,2,1,0:T(8,128)S(1)}, f32[2,2,256,256]{3,2,1,0:T(8,128)}, u32[]{:S(2)}, u32[]{:S(2)}) %collective-permute-start.2) | collective-permute-done | bytes 1048608 | tf_op jit(solution)/shard_map/ppermute | solution.py:31
  175.9 1.5 broadcast_select_fusion.3
  177.4 1.3 collective-permute-start.3
  178.7 25.6 %collective-permute-done.3 = f32[2,2,256,256]{3,2,1,0:T(8,128)} collective-permute-done((f32[2,2,256,256]{3,2,1,0:T(8,128)S(1)}, f32[2,2,256,256]{3,2,1,0:T(8,128)}, u32[]{:S(2)}, u32[]{:S(2)}) %collective-permute-start.3) | collective-permute-done | bytes 1048608 | tf_op jit(solution)/shard_map/ppermute | solution.py:31
  204.3 1.5 broadcast_select_fusion.2
  205.8 1.3 collective-permute-start.4
  207.2 101.8 %collective-permute-done.4 = f32[2,2,256,256]{3,2,1,0:T(8,128)} collective-permute-done((f32[2,2,256,256]{3,2,1,0:T(8,128)S(1)}, f32[2,2,256,256]{3,2,1,0:T(8,128)}, u32[]{:S(2)}, u32[]{:S(2)}) %collective-permute-start.4) | collective-permute-done | bytes 1048608 | tf_op jit(solution)/shard_map/ppermute | solution.py:31
  309.0 2.5 broadcast_select_fusion.1
  311.5 66.8 %conditional.8 = (f32[2,2,256,256]{3,2,1,0:T(8,128)}) conditional(s32[]{:T(128)} %convert_element_type.229, f32[2,2,256,256]{3,2,1,0:T(8,128)} %broadcast_select_fusion.1, (s32[4]{0:T(128)S(1)}, s32[]{:T(128)}, bf16[256,256]{1,0:T(8,128)(2,1)S(1)}, bf16[256,256]{1,0:T(8,128)(2,1)S(1)}, s32[]{:T(128)}, /*index=5*/f32[4,256,1152]{2,1,0:T(8,128)}, ...), branch_computations={%region_16.17_spmd, %region_17.20_spmd} | conditional | flops 1080033280 | bytes 39060652 | solution.py:166
  313.0 65.0 %while.66 = (s32[]{:T(128)}, f32[2,2,256,256]{3,2,1,0:T(8,128)}, s32[]{:T(128)}, f32[4,256,1152]{2,1,0:T(8,128)}, s32[2]{0:T(128)S(1)}, /*index=5*/bf16[256,256]...) while((s32[]{:T(128)}, f32[2,2,256,256]{3,2,1,0:T(8,128)}, ...), condition=%wide.region_19.19_spmd, body=%wide.region_18.18_spmd.sunk | while | flops 1079902208 | bytes 38536176 | solution.py:151
  313.9 1.4 dynamic-slice_bitcast_fusion.22
  315.4 4.7 %while.71 = (s32[]{:T(128)}, f32[256,1152]{1,0:T(8,128)S(1)}, s32[2,2]{1,0:T(2,128)S(1)}, f32[2,256,256]{1,2,0:T(8,128)}, s32[]{:T(128)}) while((s32[]{:T(128)}, f32[256,1152]{1,0:T(8,128)S(1)}, s32[2,2]{1,0:T(2,128)S(1)}, f32[2,256,256]{1,2,0:T(8,128)}, s32[]{:T(128)}) %tuple.295), condition=%wide.while_cond.3, body=%wide.while_body.3.sunk | while | flops 2 | bytes 1573469 | solution.py:140
  320.2 1.6 copy.275
  321.8 2.1 fusion.257
  328.1 1.1 pad_maximum_fusion.128
  329.9 1.4 dynamic-slice_bitcast_fusion.22
  331.4 4.7 %while.71 = (s32[]{:T(128)}, f32[256,1152]{1,0:T(8,128)S(1)}, s32[2,2]{1,0:T(2,128)S(1)}, f32[2,256,256]{1,2,0:T(8,128)}, s32[]{:T(128)}) while((s32[]{:T(128)}, f32[256,1152]{1,0:T(8,128)S(1)}, s32[2,2]{1,0:T(2,128)S(1)}, f32[2,256,256]{1,2,0:T(8,128)}, s32[]{:T(128)}) %tuple.295), condition=%wide.while_cond.3, body=%wide.while_body.3.sunk | while | flops 2 | bytes 1573469 | solution.py:140
  336.2 1.6 copy.275
  337.8 2.1 fusion.257
  344.1 1.1 pad_maximum_fusion.128
  345.9 1.4 dynamic-slice_bitcast_fusion.22
  347.5 4.7 %while.71 = (s32[]{:T(128)}, f32[256,1152]{1,0:T(8,128)S(1)}, s32[2,2]{1,0:T(2,128)S(1)}, f32[2,256,256]{1,2,0:T(8,128)}, s32[]{:T(128)}) while((s32[]{:T(128)}, f32[256,1152]{1,0:T(8,128)S(1)}, s32[2,2]{1,0:T(2,128)S(1)}, f32[2,256,256]{1,2,0:T(8,128)}, s32[]{:T(128)}) %tuple.295), condition=%wide.while_cond.3, body=%wide.while_body.3.sunk | while | flops 2 | bytes 1573469 | solution.py:140
  352.2 1.6 copy.275
  353.9 2.1 fusion.257
  360.2 1.1 pad_maximum_fusion.128
  362.0 1.4 dynamic-slice_bitcast_fusion.22
  363.5 4.7 %while.71 = (s32[]{:T(128)}, f32[256,1152]{1,0:T(8,128)S(1)}, s32[2,2]{1,0:T(2,128)S(1)}, f32[2,256,256]{1,2,0:T(8,128)}, s32[]{:T(128)}) while((s32[]{:T(128)}, f32[256,1152]{1,0:T(8,128)S(1)}, s32[2,2]{1,0:T(2,128)S(1)}, f32[2,256,256]{1,2,0:T(8,128)}, s32[]{:T(128)}) %tuple.295), condition=%wide.while_cond.3, body=%wide.while_body.3.sunk | while | flops 2 | bytes 1573469 | solution.py:140
  368.3 1.6 copy.275
  369.9 2.1 fusion.257
  376.2 1.1 pad_maximum_fusion.128
  378.3 1.4 collective-permute-start.5
  382.7 1.3 copy.369
  384.7 19.8 %collective-permute-done.5 = f32[2,2,256,256]{3,2,1,0:T(8,128)S(1)} collective-permute-done((f32[2,2,256,256]{3,2,1,0:T(8,128)}, f32[2,2,256,256]{3,2,1,0:T(8,128)S(1)}, u32[]{:S(2)}, u32[]{:S(2)}) %collective-permute-start.5) | collective-permute-done | bytes 1048608 | tf_op jit(solution)/shard_map/ppermute | solution.py:31
  404.6 58.6 %conditional.9 = (f32[2,2,256,256]{3,2,1,0:T(8,128)S(1)}) conditional(s32[]{:T(128)} %convert_element_type.230, f32[2,2,256,256]{3,2,1,0:T(8,128)S(1)} %broadcast_select_fusion, (s32[4]{0:T(128)S(1)}, s32[]{:T(128)}, bf16[256,256]{1,0:T(8,128)(2,1)S(1)}, bf16[256,256]{1,0:T(8,128)(2,1)S(1)}, s32[]{:T(128)}, /*index=5*/f32[4,256,1152]{2,1,0:T(8,128)}, ...), branch_computations={%region_20.21_spmd, %region_21.24_spmd} | conditional | flops 1080033280 | bytes 39060652 | solution.py:166
  406.1 57.2 %while.69 = (s32[]{:T(128)}, f32[2,2,256,256]{3,2,1,0:T(8,128)S(1)}, s32[]{:T(128)}, f32[4,256,1152]{2,1,0:T(8,128)}, s32[2]{0:T(128)S(1)}, /*index=5*/bf16[256,...) while((s32[]{:T(128)}, ...), condition=%wide.region_23.23_spmd, body=%wide.region_22.22_spmd.sunk | while | flops 1079902208 | bytes 38536176 | solution.py:151
  406.7 1.4 dynamic-slice_bitcast_fusion.20
  408.3 4.5 while.70
  413.8 2.1 fusion.242
  420.9 1.4 dynamic-slice_bitcast_fusion.20
  422.4 4.5 while.70
  428.0 2.1 fusion.242
  435.0 1.4 dynamic-slice_bitcast_fusion.20
  436.5 4.5 while.70
  442.1 2.1 fusion.242
  449.1 1.4 dynamic-slice_bitcast_fusion.20
  450.7 4.5 while.70
  456.3 2.1 fusion.242
  463.3 2.3 bitcast_dynamic-update-slice_fusion
  (315 shorter events, 87.7 us)
Async XLA Ops:
  3.5 32.1 %all-to-all-start = ((s32[32,6,1]{1,2,0:T(1,128)}), s32[32,6,1]{1,2,0:T(1,128)S(1)}, u32[]{:S(2)}, u32[]{:S(2)}) async-start(s32[32,6,1]{1,2,0:T(1,128)} %bitcast.125), calls=%async_computation | async-start | bytes 32768 | tf_op jit(solution)/shard_map/all_to_all | solution.py:123
  35.5 81.1 %all-to-all-start.1 = ((bf16[192,128,128]{2,1,0:T(8,128)(2,1)}), bf16[192,128,128]{2,1,0:T(8,128)(2,1)}, u32[]{:S(2)}, u32[]{:S(2)}) async-start(bf16[192,128,128]{2,1,0:T(8,128)(2,1)} %scatter_fusion), calls=%async_computation.1 | async-start | bytes 12582912 | tf_op jit(solution)/shard_map/all_to_all | solution.py:122
  126.1 6.4 %copy-start.7 = (f32[2,256,256]{2,1,0:T(8,128)S(1)}, f32[2,256,256]{2,1,0:T(8,128)}, u32[]{:S(2)}) copy-start(f32[2,256,256]{2,1,0:T(8,128)} %param.30) | copy-start | bytes 1572868
  127.6 14.7 %collective-permute-start = (f32[4,64,1024]{2,1,0:T(8,128)}, f32[4,64,1024]{2,1,0:T(8,128)}, u32[]{:S(2)}, u32[]{:S(2)}) collective-permute-start(f32[4,64,1024]{2,1,0:T(8,128)} %get-tuple-element.1091), channel_id=1, source_target_pairs={{0,1},{1,2},{2,3},{3,4},{4,5},{5,6},{6,7},{7,8},{8,9},{9,10},{10,1... | collective-permute-start | bytes 3145736 | tf_op jit(solution)/shard_map/ppermute | solution.py:22
  127.6 16.2 %collective-permute-start.1 = (f32[4,64,1024]{2,1,0:T(8,128)}, f32[4,64,1024]{2,1,0:T(8,128)}, u32[]{:S(2)}, u32[]{:S(2)}) collective-permute-start(f32[4,64,1024]{2,1,0:T(8,128)} %get-tuple-element.1090), channel_id=1, source_target_pairs={{1,0},{2,1},{3,2},{4,3},{5,4},{6,5},{7,6},{8,7},{9,8},{10,9},{11,1... | collective-permute-start | bytes 3145736 | tf_op jit(solution)/shard_map/ppermute | solution.py:23
  145.2 2.7 copy-start.24
  148.1 29.3 %copy-start.4 = (f32[2,2,256,256]{3,2,1,0:T(8,128)}, f32[2,2,256,256]{3,2,1,0:T(8,128)S(1)}, u32[]{:S(2)}) copy-start(f32[2,2,256,256]{3,2,1,0:T(8,128)S(1)} %get-tuple-element.2198) | copy-start | bytes 3145732
  148.1 27.8 %collective-permute-start.2 = (f32[2,2,256,256]{3,2,1,0:T(8,128)S(1)}, f32[2,2,256,256]{3,2,1,0:T(8,128)}, u32[]{:S(2)}, u32[]{:S(2)}) collective-permute-start(f32[2,2,256,256]{3,2,1,0:T(8,128)S(1)} %get-tuple-element.2198), channel_id=1, source_target_pairs={{0,32},{32,64},{64,96},{1,33},{33,65},{65,97},{2,34},{34,66},{66,9... | collective-permute-start | bytes 3145736 | tf_op jit(solution)/shard_map/ppermute | solution.py:31
  177.4 26.9 %collective-permute-start.3 = (f32[2,2,256,256]{3,2,1,0:T(8,128)S(1)}, f32[2,2,256,256]{3,2,1,0:T(8,128)}, u32[]{:S(2)}, u32[]{:S(2)}) collective-permute-start(f32[2,2,256,256]{3,2,1,0:T(8,128)S(1)} %get-tuple-element.2199), channel_id=1, source_target_pairs={{0,32},{32,64},{64,96},{1,33},{33,65},{65,97},{2,34},{34,66},{66,9... | collective-permute-start | bytes 3145736 | tf_op jit(solution)/shard_map/ppermute | solution.py:31
  205.8 105.7 %copy-start.1 = (f32[2,2,256,256]{3,2,1,0:T(8,128)}, f32[2,2,256,256]{3,2,1,0:T(8,128)S(1)}, u32[]{:S(2)}) copy-start(f32[2,2,256,256]{3,2,1,0:T(8,128)S(1)} %get-tuple-element.2200) | copy-start | bytes 3145732
  205.8 103.2 %collective-permute-start.4 = (f32[2,2,256,256]{3,2,1,0:T(8,128)S(1)}, f32[2,2,256,256]{3,2,1,0:T(8,128)}, u32[]{:S(2)}, u32[]{:S(2)}) collective-permute-start(f32[2,2,256,256]{3,2,1,0:T(8,128)S(1)} %get-tuple-element.2200), channel_id=1, source_target_pairs={{0,32},{32,64},{64,96},{1,33},{33,65},{65,97},{2,34},{34,66},{66,9... | collective-permute-start | bytes 3145736 | tf_op jit(solution)/shard_map/ppermute | solution.py:31
  320.2 1.6 copy-start.12
  325.4 0.9 copy-start.20
  326.7 0.9 copy-start.21
  336.2 1.6 copy-start.12
  341.5 0.9 copy-start.20
  342.7 0.9 copy-start.21
  352.2 1.6 copy-start.12
  357.5 0.9 copy-start.20
  358.8 0.9 copy-start.21
  368.3 1.6 copy-start.12
  373.5 0.9 copy-start.20
  374.8 0.9 copy-start.21
  378.3 1.6 copy-start.5
  378.3 26.2 %collective-permute-start.5 = (f32[2,2,256,256]{3,2,1,0:T(8,128)}, f32[2,2,256,256]{3,2,1,0:T(8,128)S(1)}, u32[]{:S(2)}, u32[]{:S(2)}) collective-permute-start(f32[2,2,256,256]{3,2,1,0:T(8,128)} %get-tuple-element.2201), channel_id=1, source_target_pairs={{0,32},{32,64},{64,96},{1,33},{33,65},{65,97},{2,34},{34,66},{66,9... | collective-permute-start | bytes 3145736 | tf_op jit(solution)/shard_map/ppermute | solution.py:31
  380.0 1.2 copy-start.2
  381.3 1.2 copy-start.3
  382.7 2.0 copy-start.6
  382.7 21.8 %copy-start.8 = (f32[2,256,256]{2,1,0:T(8,128)S(1)}, f32[2,256,256]{2,1,0:T(8,128)}, u32[]{:S(2)}) copy-start(f32[2,256,256]{2,1,0:T(8,128)} %param.30) | copy-start | bytes 1572868
  412.8 1.0 copy-start.13
  417.4 0.9 copy-start.22
  418.7 0.9 copy-start.23
  426.9 1.0 copy-start.13
  431.6 0.9 copy-start.22
  432.8 0.9 copy-start.23
  441.1 1.0 copy-start.13
  445.7 0.9 copy-start.22
  447.0 0.9 copy-start.23
  455.2 1.0 copy-start.13
  459.9 0.9 copy-start.22
  461.1 0.9 copy-start.23
where the time goes:
time: 469 us; the launch traced here: 466 us
  waiting for transfers between devices  256 us (55%)
  local copies, waits for them, and re-layouts  103 us (22%)
  other arithmetic  44.6 us (10%)
  matrix products  29.7 us (6%)
  starting transfers between devices  23.1 us (5%)
  loops' own time  8.54 us (2%)
    ppermute x4, waiting for transfers between devices, shifted(): return lax.ppermute(block, axis, route)  174 us
    all_to_all x1, waiting for transfers between devices, shards(): lax.all_to_all(outgoing, 'probe', split_axis=0, concat_axis=0, tiled=True)  72.3 us
    gather x80, local copies, waits for them, and re-layouts  36.8 us
    another operation x32, other arithmetic  21.1 us
    scatter x1, local copies, waits for them, and re-layouts, shards(): jnp.zeros((owners * capacity, tile_size, tile_size), jnp.bfloat16)  19.3 us
    squeeze x8, local copies, waits for them, and re-layouts, crop_all(): plane = lax.dynamic_index_in_dim(wrapped, slice_index, 0, keepdims=False)  10.8 us
    ppermute x1, waiting for transfers between devices, extended_2(): before = lax.ppermute(last, axis, up)  9.76 us
  transfers between devices with their start and end apart: 8, of which 6 were waited for; matrix products, arithmetic and copies ran while one was open for 7% of the time, Pallas kernels for 0%

commit v1 on v0

v1 whole, which is shorter than its diff:
```python
import functools
import math

import jax
import jax.numpy as jnp
from jax import lax
from jax.experimental import pallas as pl
from jax.experimental.pallas import tpu as pltpu
from jax.sharding import PartitionSpec as P

SLICE_MAX = 4
TCOLS = 8
TILES = SLICE_MAX * TCOLS
TILE = 128
N = 256
SIGMA = 0.7
CAP = 6
META = 16
POS_LANE = 8
CHUNKS = 2
ROWS = TILE // CHUNKS
SKIP = 64.0

BF16 = jnp.bfloat16
F32 = jnp.float32


def dft_tables(points):
    grid_index = jnp.arange(points, dtype=jnp.int32)
    angle_table = (grid_index[:, None] * grid_index[None, :] % points).astype(F32) * (
        2.0 * math.pi / points
    )
    norm_scale = 1.0 / math.sqrt(points)
    real_part = (jnp.cos(angle_table) * norm_scale).astype(BF16)
    imag_part = (-jnp.sin(angle_table) * norm_scale).astype(BF16)
    return (real_part, imag_part)


def whole(space=pltpu.VMEM):
    return pl.BlockSpec(memory_space=space)


def pack_kernel(row0, tile_sm, pos_sm, blocks_hbm, tile_row, tile_col, out, counts, sem):
    owners, rows_all, _ = out.shape
    atoms = tile_row.shape[1]

    @pl.loop(0, owners)
    def _(o):
        counts[o] = 0

    @pl.loop(0, atoms)
    def _(a):
        o = tile_sm[a] // TILES
        r = counts[o]
        counts[o] = r + 1
        pltpu.make_async_copy(
            blocks_hbm.at[a, pl.ds(row0, ROWS), :],
            out.at[o, pl.ds(pl.multiple_of(r * ROWS, ROWS), ROWS), :],
            sem,
        ).start()

    t_row = tile_row[...]
    t_col = tile_col[...]
    own_row = t_row // TILES
    own_col = t_col // TILES
    shape = (atoms, atoms)
    i_sub = lax.broadcasted_iota(jnp.int32, shape, 0)
    i_lane = lax.broadcasted_iota(jnp.int32, shape, 1)
    earlier = jnp.where((own_row == own_col) & (i_lane < i_sub), 1.0, 0.0)
    rank_col = jnp.sum(earlier, axis=1, keepdims=True).astype(jnp.int32)
    slot_of = jnp.where(rank_col == i_lane, (t_col % TILES + 1).astype(F32), 0.0).astype(BF16)
    o_sub = lax.broadcasted_iota(jnp.int32, (owners, atoms), 0)
    o_lane = lax.broadcasted_iota(jnp.int32, (owners, atoms), 1)
    named = jnp.where(own_row == o_sub, 1.0, 0.0).astype(BF16)
    meta = jnp.dot(named, slot_of, preferred_element_type=F32)
    for k in range(pos_sm.shape[0]):
        meta = jnp.where(o_lane == POS_LANE + k, pos_sm[k].astype(F32), meta)
    for o in range(owners):
        line = jnp.broadcast_to(meta[o : o + 1, :], (META, atoms))
        out[o, pl.ds(CAP * ROWS, META), :] = line.astype(BF16)
    pltpu.make_async_copy(
        blocks_hbm.at[:, pl.ds(row0, ROWS), :], blocks_hbm.at[:, pl.ds(row0, ROWS), :], sem
    ).wait()


def pack(blocks, tiles, positions, chunk, owners):
    atoms = blocks.shape[0]
    return pl.pallas_call(
        functools.partial(pack_kernel, chunk * ROWS),
        out_shape=jax.ShapeDtypeStruct((owners, CAP * ROWS + META, TILE), BF16),
        in_specs=[whole(pltpu.SMEM), whole(pltpu.SMEM), whole(pl.ANY), whole(), whole()],
        out_specs=whole(),
        scratch_shapes=[pltpu.SMEM((owners,), jnp.int32), pltpu.SemaphoreType.DMA],
        name=f"pack{chunk}",
    )(tiles, positions, blocks, tiles.reshape(1, atoms), tiles.reshape(atoms, 1))


TWO_PI_HI = 6.28125
TWO_PI_LO = 2.0 * math.pi - TWO_PI_HI


def gather_kernel(upper, slices_sm, place_sm, arrived, own, halo, acc, meta_v, meta_s, sem):
    owners = arrived.shape[0]
    waves = own.shape[0]
    meta_v[...] = arrived[:, CAP * ROWS, :].astype(F32).astype(jnp.int32)
    copy = pltpu.make_async_copy(meta_v, meta_s, sem)
    copy.start()
    acc[...] = jnp.zeros_like(acc)
    copy.wait()

    @pl.loop(0, owners)
    def _(o):
        for r in range(CAP):
            t = meta_s[o, r]

            @pl.when(t > 0)
            def _():
                acc[t - 1] += arrived[o, pl.ds(r * ROWS, ROWS), :].astype(F32)

    count = slices_sm[0]
    me = place_sm[0]
    ahead = place_sm[1]

    def phase(tile):
        angle = SIGMA * acc[tile]
        turns = jnp.round(angle * (1.0 / (2.0 * math.pi)))
        return ((angle - turns * TWO_PI_HI) - turns * TWO_PI_LO).astype(BF16)

    for target, ref in ((me, own), (ahead, halo)):
        for d in range(waves):
            start = meta_s[target, POS_LANE + d]
            for h in range(2):
                column = lax.rem(start + h, TCOLS)

                @pl.loop(0, SLICE_MAX)
                def _(s):
                    value = phase(s * TCOLS + column)
                    ref[d, s, h] = jnp.where(s < count, value, jnp.full_like(value, SKIP))


def gather(arrived, slice_count, place, upper, waves, chunk):
    shape = jax.ShapeDtypeStruct((waves, SLICE_MAX, 2, ROWS, TILE), BF16)
    owners = arrived.shape[0]
    return pl.pallas_call(
        functools.partial(gather_kernel, upper),
        out_shape=(shape, shape),
        in_specs=[whole(pltpu.SMEM), whole(pltpu.SMEM), whole()],
        out_specs=(whole(), whole()),
        scratch_shapes=[
            pltpu.VMEM((TILES, ROWS, TILE), F32),
            pltpu.VMEM((owners, TILE), jnp.int32),
            pltpu.SMEM((owners, TILE), jnp.int32),
            pltpu.SemaphoreType.DMA,
        ],
        name=f"gather{chunk}",
    )(slice_count, place, arrived)


SIN_C = (-1.6666654611e-1, 8.3321608736e-3, -1.9515295891e-4)
COS_C = (4.166664568298827e-2, -1.388731625493765e-3, 2.443315711809948e-5)


def sin_cos(angle):
    quarter = jnp.round(angle * (2.0 / math.pi))
    x = angle - quarter * (math.pi / 2.0)
    x2 = x * x
    s = x + x * x2 * (SIN_C[0] + x2 * (SIN_C[1] + x2 * SIN_C[2]))
    c = 1.0 - 0.5 * x2 + x2 * x2 * (COS_C[0] + x2 * (COS_C[1] + x2 * COS_C[2]))
    odd = jnp.abs(quarter) == 1.0
    sin_out = jnp.where(odd, c, s)
    cos_out = jnp.where(odd, s, c)
    sin_out = jnp.where((quarter == -1.0) | (jnp.abs(quarter) == 2.0), -sin_out, sin_out)
    cos_out = jnp.where((quarter == 1.0) | (jnp.abs(quarter) == 2.0), -cos_out, cos_out)
    return sin_out, cos_out


def waves_kernel(sections, wave_ref, phase_ref, m1, m2, *refs):
    windows = refs[: 2 * CHUNKS]
    out, psi, left, mid, rotor = refs[2 * CHUNKS :]
    step = 32

    for b in range(N // step):
        rows = pl.ds(b * step, step)
        for c in range(2):
            psi[rows, pl.ds(c * N, N)] = wave_ref[c, rows, :]
        angle = phase_ref[rows, :]
        s_out, c_out = sin_cos(angle)
        rotor[rows, pl.ds(0, N)] = c_out
        rotor[rows, pl.ds(N, N)] = s_out

    def place_of(row):
        if row < TILE // 2:
            tile_row, base = row + TILE // 2, CHUNKS
        elif row < TILE // 2 + TILE:
            tile_row, base = row - TILE // 2, 0
        else:
            tile_row, base = row - TILE // 2 - TILE, CHUNKS
        return windows[base + tile_row // ROWS], tile_row % ROWS

    def one_slice(sec, s):
        for b in range(N // step):
            ref, row = place_of(b * step)
            rows = pl.ds(b * step, step)
            for h in range(2):
                angle = ref[sec, s, h, pl.ds(row, step), :].astype(F32)
                s_out, c_out = sin_cos(angle)
                re = psi[rows, pl.ds(h * TILE, TILE)]
                im = psi[rows, pl.ds(N + h * TILE, TILE)]
                lanes = pl.ds(h * TILE, TILE)
                left[rows, lanes] = (re * c_out - im * s_out).astype(BF16)
                left[pl.ds(N + b * step, step), lanes] = (re * s_out + im * c_out).astype(BF16)
        for c in range(2):
            half = jnp.dot(m1[pl.ds(c * N, N), :], left[...], preferred_element_type=F32)
            mid[:, pl.ds(c * N, N)] = half.astype(BF16)
        for b in range(2):
            half = N // 2
            rows = pl.ds(b * half, half)
            value = jnp.dot(mid[rows, :], m2[...], preferred_element_type=F32)
            re, im = value[:, :N], value[:, N:]
            cr, ci = rotor[rows, pl.ds(0, N)], rotor[rows, pl.ds(N, N)]
            left[rows, :] = (re * cr - im * ci).astype(BF16)
            left[pl.ds(N + b * half, half), :] = (re * ci + im * cr).astype(BF16)
        for c in range(2):
            half = jnp.dot(m2[pl.ds(c * N, N), :], left[...], preferred_element_type=F32)
            mid[:, pl.ds(c * N, N)] = half.astype(BF16)
        for b in range(2):
            half = N // 2
            rows = pl.ds(b * half, half)
            psi[rows, :] = jnp.dot(mid[rows, :], m1[...], preferred_element_type=F32)

    @pl.loop(0, sections)
    def _(sec):
        @pl.loop(0, SLICE_MAX)
        def _(s):
            used = jnp.max(windows[0][sec, s, 0, pl.ds(0, 16), :].astype(F32)) < SKIP / 2

            @pl.when(used)
            def _():
                one_slice(sec, s)

        for c in range(2):
            out[sec, c] = psi[:, pl.ds(c * N, N)].astype(BF16)


def run_waves(probe_wave, prop_phase, m1, m2, windows):
    sections = windows[0].shape[0]
    return pl.pallas_call(
        functools.partial(waves_kernel, sections),
        out_shape=jax.ShapeDtypeStruct((sections, 2, N, N), BF16),
        in_specs=[whole()] * (4 + len(windows)),
        out_specs=whole(),
        scratch_shapes=[
            pltpu.VMEM((N, 2 * N), F32),
            pltpu.VMEM((2 * N, N), BF16),
            pltpu.VMEM((N, 2 * N), BF16),
            pltpu.VMEM((N, 2 * N), F32),
        ],
        name="waves",
    )(probe_wave, prop_phase, m1, m2, *windows)


def shards(atom_blocks, atom_tile, slice_counts, positions, probe_wave, prop_phase):
    owners = lax.axis_size("probe")
    waves = positions.shape[0]
    me = lax.axis_index("probe")
    blocks = atom_blocks[0]
    tiles = atom_tile[0]
    up = [(i, (i + 1) % owners) for i in range(owners)]
    down = [(j, i) for i, j in up]
    own, halo = [], []
    for chunk in range(CHUNKS):
        upper = chunk * ROWS >= TILE // 2
        ahead = lax.rem(me + (1 if upper else owners - 1), owners)
        place = jnp.stack([me, ahead]).astype(jnp.int32)
        packed = pack(blocks, tiles, positions, chunk, owners)
        arrived = lax.all_to_all(packed, "probe", split_axis=0, concat_axis=0, tiled=True)
        mine, theirs = gather(arrived, slice_counts, place, upper, waves, chunk)
        mine = lax.all_to_all(mine, "depth", split_axis=0, concat_axis=0, tiled=True)
        theirs = lax.ppermute(theirs, "probe", up if upper else down)
        theirs = lax.all_to_all(theirs, "depth", split_axis=0, concat_axis=0, tiled=True)
        own.append(mine)
        halo.append(theirs)
    fr, fi = dft_tables(N)
    m1 = jnp.concatenate(
        [jnp.concatenate([fr, -fi], axis=1), jnp.concatenate([fi, fr], axis=1)], axis=0
    )
    m2 = jnp.concatenate(
        [jnp.concatenate([fr, fi], axis=1), jnp.concatenate([-fi, fr], axis=1)], axis=0
    )
    left = run_waves(probe_wave, prop_phase, m1, m2, own + halo)
    left = lax.all_to_all(left, "depth", split_axis=0, concat_axis=0, tiled=True)
    return left.astype(F32)[None]


def solution(mesh):
    in_specs = (
        P("depth", "probe", None, None),
        P("depth", "probe"),
        P("depth"),
        P("probe"),
        P(),
        P(),
    )
    out_specs = P("depth", "probe", None, None, None)
    return jax.shard_map(shards, mesh=mesh, in_specs=in_specs, out_specs=out_specs, check_vma=False)
```

time: 469 us -> 198 us (0.42)
  the two profiles are of different devices: /device:TPU:22 before, /device:TPU:0 now
where the time goes in v1:
time: 198 us; the launch traced here: 195 us
  waiting for transfers between devices  96.4 us (49%)
  Pallas kernels  43.6 us (22%)
  starting transfers between devices  28.9 us (15%)
  blocking collectives  15.9 us (8%)
  other arithmetic  5.91 us (3%)
  local copies, waits for them, and re-layouts  3.91 us (2%)
    all_to_all x2, waiting for transfers between devices, shards(): lax.all_to_all(packed, 'probe', split_axis=0, concat_axis=0, tiled=True)  72.7 us
    pallas_call x1, Pallas kernels, run_waves(): pl.pallas_call(functools.partial(waves_kernel, sections), out_shape=jax.S...  17.6 us
    all_to_all x1, blocking collectives, shards(): lax.all_to_all(left, 'depth', split_axis=0, concat_axis=0, tiled=True)  15.9 us
    pallas_call x2, Pallas kernels, gather(): pl.pallas_call(functools.partial(gather_kernel, upper), out_shape=(shape,...  14.4 us
    all_to_all x2, waiting for transfers between devices, shards(): lax.all_to_all(theirs, 'depth', split_axis=0, concat_axis=0, tiled=True)  13.9 us
    all_to_all x2, starting transfers between devices, shards(): lax.all_to_all(packed, 'probe', split_axis=0, concat_axis=0, tiled=True)  12.5 us
    pallas_call x2, Pallas kernels, pack(): pl.pallas_call(functools.partial(pack_kernel, chunk * ROWS), out_shape=ja...  11.6 us
    all_to_all x2, waiting for transfers between devices, shards(): lax.all_to_all(mine, 'depth', split_axis=0, concat_axis=0, tiled=True)  9.83 us
  transfers between devices with their start and end apart: 8, of which 5 were waited for; matrix products, arithmetic and copies ran while one was open for 2% of the time, Pallas kernels for 10%

profile of v1, /device:TPU:0, one launch (start us, length us, event | category | flops | bytes accessed | tf_op | source)
XLA Modules:
  0.0 195.4 jit_solution(13128949751460671801)
XLA Ops:
  0.0 1.4 copy.7.tile_col
  1.4 5.9 %pack0.1 = bf16[32,400,128]{2,1,0:T(8,128)(2,1)} custom-call(s32[128]{0:T(128)} %bitcast.12, s32[4]{0:T(128)} %pos_sm.3, bf16[128,128,128]{2,1,0:T(8,128)(2,1)} %bitcast.9, s32[1,128]{1,0:T(1,128)} %tile_row.3, s32[128,1]{1,0:T(8,128)} %copy.7.tile_col), custom_call_target="tpu_custom_call" | custom-call | tf_op jit(solution)/shard_map/pack0/pallas_call | solution.py:88
  7.2 8.5 %all-to-all-start = ((bf16[32,400,128]{2,1,0:T(8,128)(2,1)}), bf16[32,400,128]{2,1,0:T(8,128)(2,1)S(1)}, u32[]{:S(2)}, u32[]{:S(2)}) async-start(bf16[32,400,128]{2,1,0:T(8,128)(2,1)} %pack0.1), calls=%async_computation | async-start | bytes 6553600 | tf_op jit(solution)/shard_map/all_to_all | solution.py:276
  15.7 5.8 %pack1.1 = bf16[32,400,128]{2,1,0:T(8,128)(2,1)} custom-call(s32[128]{0:T(128)} %bitcast.13, s32[4]{0:T(128)} %pos_sm.3, bf16[128,128,128]{2,1,0:T(8,128)(2,1)} %bitcast.10, s32[1,128]{1,0:T(1,128)} %tile_row.3, s32[128,1]{1,0:T(8,128)} %copy.7.tile_col), custom_call_target="tpu_custom_call" | custom-call | tf_op jit(solution)/shard_map/pack1/pallas_call | solution.py:88
  21.5 37.7 %all-to-all-done.arrived = bf16[32,400,128]{2,1,0:T(8,128)(2,1)S(1)} async-done(((bf16[32,400,128]{2,1,0:T(8,128)(2,1)}), bf16[32,400,128]{2,1,0:T(8,128)(2,1)S(1)}, u32[]{:S(2)}, u32[]{:S(2)}) %all-to-all-start) | async-done | bytes 3276832 | tf_op jit(solution)/shard_map/all_to_all | solution.py:276
  59.2 0.0 copy-start.1
  59.2 1.7 copy-done.1
  60.9 4.1 %all-to-all-start.2 = ((bf16[32,400,128]{2,1,0:T(8,128)(2,1)}), bf16[32,400,128]{2,1,0:T(8,128)(2,1)S(1)}, u32[]{:S(2)}, u32[]{:S(2)}) async-start(bf16[32,400,128]{2,1,0:T(8,128)(2,1)} %pack1.1), calls=%async_computation.2 | async-start | bytes 6553600 | tf_op jit(solution)/shard_map/all_to_all | solution.py:276
  65.6 0.7 pad_add_fusion.place_sm
  66.3 7.2 %gather0.1 = (bf16[4,4,2,64,128]{4,3,2,1,0:T(8,128)(2,1)}, bf16[4,4,2,64,128]{4,3,2,1,0:T(8,128)(2,1)}) custom-call(s32[1]{0:T(128)S(6)} %copy.9.slices_sm, s32[2]{0:T(128)} %pad_add_fusion.place_sm, bf16[32,400,128]{2,1,0:T(8,128)(2,1)} %copy-done.1), custom_call_target="tpu_custom_call" | custom-call | tf_op jit(solution)/shard_map/gather0/pallas_call | solution.py:144
  73.5 35.0 %all-to-all-done.2.arrived = bf16[32,400,128]{2,1,0:T(8,128)(2,1)S(1)} async-done(((bf16[32,400,128]{2,1,0:T(8,128)(2,1)}), bf16[32,400,128]{2,1,0:T(8,128)(2,1)S(1)}, u32[]{:S(2)}, u32[]{:S(2)}) %all-to-all-start.2) | async-done | bytes 3276832 | tf_op jit(solution)/shard_map/all_to_all | solution.py:276
  108.5 0.0 copy-start
  108.5 4.3 %all-to-all-start.1 = ((bf16[4,4,2,64,128]{4,3,2,1,0:T(8,128)(2,1)}), bf16[4,4,2,64,128]{4,3,2,1,0:T(8,128)(2,1)}, u32[]{:S(2)}, u32[]{:S(2)}) async-start(bf16[4,4,2,64,128]{4,3,2,1,0:T(8,128)(2,1)} %get-tuple-element.9), calls=%async_computation.1 | async-start | bytes 1048576 | tf_op jit(solution)/shard_map/all_to_all | solution.py:278
  112.8 0.7 collective-permute-start
  113.5 0.6 pad_add_fusion.1.place_sm
  114.1 0.0 copy-done
  114.1 7.2 %gather1.1 = (bf16[4,4,2,64,128]{4,3,2,1,0:T(8,128)(2,1)}, bf16[4,4,2,64,128]{4,3,2,1,0:T(8,128)(2,1)}) custom-call(s32[1]{0:T(128)S(6)} %copy.9.slices_sm, s32[2]{0:T(128)} %pad_add_fusion.1.place_sm, bf16[32,400,128]{2,1,0:T(8,128)(2,1)} %copy-done), custom_call_target="tpu_custom_call" | custom-call | tf_op jit(solution)/shard_map/gather1/pallas_call | solution.py:144
  121.3 0.0 all-to-all-done.1.refs_0_
  121.3 4.4 %all-to-all-start.3 = ((bf16[4,4,2,64,128]{4,3,2,1,0:T(8,128)(2,1)}), bf16[4,4,2,64,128]{4,3,2,1,0:T(8,128)(2,1)S(1)}, u32[]{:S(2)}, u32[]{:S(2)}) async-start(bf16[4,4,2,64,128]{4,3,2,1,0:T(8,128)(2,1)} %get-tuple-element.10), calls=%async_computation.3 | async-start | bytes 1048576 | tf_op jit(solution)/shard_map/all_to_all | solution.py:278
  125.7 0.0 collective-permute-start.1
  125.7 9.8 %all-to-all-done.3.refs_1_ = bf16[4,4,2,64,128]{4,3,2,1,0:T(8,128)(2,1)S(1)} async-done(((bf16[4,4,2,64,128]{4,3,2,1,0:T(8,128)(2,1)}), bf16[4,4,2,64,128]{4,3,2,1,0:T(8,128)(2,1)S(1)}, u32[]{:S(2)}, u32[]{:S(2)}) %all-to-all-start.3) | async-done | bytes 524320 | tf_op jit(solution)/shard_map/all_to_all | solution.py:278
  135.5 0.0 copy-start.2
  135.5 0.0 collective-permute-done
  135.5 3.5 %all-to-all-start.4 = ((bf16[4,4,2,64,128]{4,3,2,1,0:T(8,128)(2,1)}), bf16[4,4,2,64,128]{4,3,2,1,0:T(8,128)(2,1)S(1)}, u32[]{:S(2)}, u32[]{:S(2)}) async-start(bf16[4,4,2,64,128]{4,3,2,1,0:T(8,128)(2,1)} %collective-permute-done), calls=%async_computation.4 | async-start | bytes 1048576 | tf_op jit(solution)/shard_map/all_to_all | solution.py:280
  139.0 0.0 collective-permute-done.1
  139.0 9.0 %all-to-all-done.4.refs_2_ = bf16[4,4,2,64,128]{4,3,2,1,0:T(8,128)(2,1)S(1)} async-done(((bf16[4,4,2,64,128]{4,3,2,1,0:T(8,128)(2,1)}), bf16[4,4,2,64,128]{4,3,2,1,0:T(8,128)(2,1)S(1)}, u32[]{:S(2)}, u32[]{:S(2)}) %all-to-all-start.4) | async-done | bytes 524320 | tf_op jit(solution)/shard_map/all_to_all | solution.py:280
  148.1 0.0 copy-start.3
  148.1 3.5 %all-to-all-start.5 = ((bf16[4,4,2,64,128]{4,3,2,1,0:T(8,128)(2,1)}), bf16[4,4,2,64,128]{4,3,2,1,0:T(8,128)(2,1)S(1)}, u32[]{:S(2)}, u32[]{:S(2)}) async-start(bf16[4,4,2,64,128]{4,3,2,1,0:T(8,128)(2,1)} %collective-permute-done.1), calls=%async_computation.5 | async-start | bytes 1048576 | tf_op jit(solution)/shard_map/all_to_all | solution.py:280
  151.5 1.0 fusion.8
  152.5 1.1 multiply_convert_fusion
  153.7 1.0 fusion.1
  154.7 4.9 %all-to-all-done.5.refs_3_ = bf16[4,4,2,64,128]{4,3,2,1,0:T(8,128)(2,1)S(1)} async-done(((bf16[4,4,2,64,128]{4,3,2,1,0:T(8,128)(2,1)}), bf16[4,4,2,64,128]{4,3,2,1,0:T(8,128)(2,1)S(1)}, u32[]{:S(2)}, u32[]{:S(2)}) %all-to-all-start.5) | async-done | bytes 524320 | tf_op jit(solution)/shard_map/all_to_all | solution.py:280
  159.6 0.0 copy-start.4
  159.6 0.0 copy-done.2
  159.6 0.0 copy-done.3
  159.6 0.8 copy-done.4
  160.4 17.6 %waves.1 = bf16[4,2,256,256]{3,2,1,0:T(8,128)(2,1)} custom-call(f32[2,256,256]{2,1,0:T(8,128)} %wave_ref.1, f32[256,256]{1,0:T(8,128)} %phase_ref.1, bf16[512,512]{1,0:T(8,128)(2,1)} %get-tuple-element.14.m1, bf16[512,512]{1,0:T(8,128)(2,1)} %get-tuple-element.13.m2, bf16[4,4,2,64,128]{4,3,2,1,0:T(8,128)(2,1)} %all-to-all-done.1.refs_0_, ...), custom_call_target="tpu_custom_call" | custom-call | tf_op jit(solution)/shard_map/waves/pallas_call | solution.py:247
  178.0 15.9 %all_to_all.35 = bf16[4,2,256,256]{3,2,1,0:T(8,128)(2,1)S(1)} all-to-all(bf16[4,2,256,256]{3,2,1,0:T(8,128)(2,1)} %waves.1), channel_id=1, replica_groups=mesh['depth'=4,'probe'=32] {'depth'}, dimensions={0} | all-to-all | bytes 2097152 | tf_op jit(solution)/shard_map/all_to_all | solution.py:291
  193.9 1.5 bitcast_convert_fusion
Async XLA Ops:
  7.2 51.9 %all-to-all-start = ((bf16[32,400,128]{2,1,0:T(8,128)(2,1)}), bf16[32,400,128]{2,1,0:T(8,128)(2,1)S(1)}, u32[]{:S(2)}, u32[]{:S(2)}) async-start(bf16[32,400,128]{2,1,0:T(8,128)(2,1)} %pack0.1), calls=%async_computation | async-start | bytes 6553600 | tf_op jit(solution)/shard_map/all_to_all | solution.py:276
  59.2 1.7 copy-start.1
  60.9 47.5 %all-to-all-start.2 = ((bf16[32,400,128]{2,1,0:T(8,128)(2,1)}), bf16[32,400,128]{2,1,0:T(8,128)(2,1)S(1)}, u32[]{:S(2)}, u32[]{:S(2)}) async-start(bf16[32,400,128]{2,1,0:T(8,128)(2,1)} %pack1.1), calls=%async_computation.2 | async-start | bytes 6553600 | tf_op jit(solution)/shard_map/all_to_all | solution.py:276
  108.5 5.6 %copy-start = (bf16[32,400,128]{2,1,0:T(8,128)(2,1)}, bf16[32,400,128]{2,1,0:T(8,128)(2,1)S(1)}, u32[]{:S(2)}) copy-start(bf16[32,400,128]{2,1,0:T(8,128)(2,1)S(1)} %all-to-all-done.2.arrived) | copy-start | bytes 9830404
  108.5 12.8 %all-to-all-start.1 = ((bf16[4,4,2,64,128]{4,3,2,1,0:T(8,128)(2,1)}), bf16[4,4,2,64,128]{4,3,2,1,0:T(8,128)(2,1)}, u32[]{:S(2)}, u32[]{:S(2)}) async-start(bf16[4,4,2,64,128]{4,3,2,1,0:T(8,128)(2,1)} %get-tuple-element.9), calls=%async_computation.1 | async-start | bytes 1048576 | tf_op jit(solution)/shard_map/all_to_all | solution.py:278
  112.8 22.8 %collective-permute-start = (bf16[4,4,2,64,128]{4,3,2,1,0:T(8,128)(2,1)}, bf16[4,4,2,64,128]{4,3,2,1,0:T(8,128)(2,1)}, u32[]{:S(2)}, u32[]{:S(2)}) collective-permute-start(bf16[4,4,2,64,128]{4,3,2,1,0:T(8,128)(2,1)} %get-tuple-element.11), channel_id=1, source_target_pairs={{1,0},{2,1},{3,2},{4,3},{5,4},{6,5},{7,6},{8,7},{9,8},{10,9},{11,1... | collective-permute-start | bytes 1572872 | tf_op jit(solution)/shard_map/ppermute | solution.py:279
  121.3 14.2 %all-to-all-start.3 = ((bf16[4,4,2,64,128]{4,3,2,1,0:T(8,128)(2,1)}), bf16[4,4,2,64,128]{4,3,2,1,0:T(8,128)(2,1)S(1)}, u32[]{:S(2)}, u32[]{:S(2)}) async-start(bf16[4,4,2,64,128]{4,3,2,1,0:T(8,128)(2,1)} %get-tuple-element.10), calls=%async_computation.3 | async-start | bytes 1048576 | tf_op jit(solution)/shard_map/all_to_all | solution.py:278
  125.7 13.3 %collective-permute-start.1 = (bf16[4,4,2,64,128]{4,3,2,1,0:T(8,128)(2,1)}, bf16[4,4,2,64,128]{4,3,2,1,0:T(8,128)(2,1)}, u32[]{:S(2)}, u32[]{:S(2)}) collective-permute-start(bf16[4,4,2,64,128]{4,3,2,1,0:T(8,128)(2,1)} %get-tuple-element.12), channel_id=1, source_target_pairs={{0,1},{1,2},{2,3},{3,4},{4,5},{5,6},{6,7},{7,8},{8,9},{9,10},{10,1... | collective-permute-start | bytes 1572872 | tf_op jit(solution)/shard_map/ppermute | solution.py:279
  135.5 24.1 %copy-start.2 = (bf16[4,4,2,64,128]{4,3,2,1,0:T(8,128)(2,1)}, bf16[4,4,2,64,128]{4,3,2,1,0:T(8,128)(2,1)S(1)}, u32[]{:S(2)}) copy-start(bf16[4,4,2,64,128]{4,3,2,1,0:T(8,128)(2,1)S(1)} %all-to-all-done.3.refs_1_) | copy-start | bytes 1572868
  135.5 12.5 %all-to-all-start.4 = ((bf16[4,4,2,64,128]{4,3,2,1,0:T(8,128)(2,1)}), bf16[4,4,2,64,128]{4,3,2,1,0:T(8,128)(2,1)S(1)}, u32[]{:S(2)}, u32[]{:S(2)}) async-start(bf16[4,4,2,64,128]{4,3,2,1,0:T(8,128)(2,1)} %collective-permute-done), calls=%async_computation.4 | async-start | bytes 1048576 | tf_op jit(solution)/shard_map/all_to_all | solution.py:280
  148.1 11.5 %copy-start.3 = (bf16[4,4,2,64,128]{4,3,2,1,0:T(8,128)(2,1)}, bf16[4,4,2,64,128]{4,3,2,1,0:T(8,128)(2,1)S(1)}, u32[]{:S(2)}) copy-start(bf16[4,4,2,64,128]{4,3,2,1,0:T(8,128)(2,1)S(1)} %all-to-all-done.4.refs_2_) | copy-start | bytes 1572868
  148.1 11.5 %all-to-all-start.5 = ((bf16[4,4,2,64,128]{4,3,2,1,0:T(8,128)(2,1)}), bf16[4,4,2,64,128]{4,3,2,1,0:T(8,128)(2,1)S(1)}, u32[]{:S(2)}, u32[]{:S(2)}) async-start(bf16[4,4,2,64,128]{4,3,2,1,0:T(8,128)(2,1)} %collective-permute-done.1), calls=%async_computation.5 | async-start | bytes 1048576 | tf_op jit(solution)/shard_map/all_to_all | solution.py:280
  159.6 0.8 copy-start.4
